TPU v7x, 512 devices: a whole 4x8x8 slice. The times are simulated.
512 devices in a mesh: dp: 8 (over z), expert: 64 (over y, x, core).
Axes of the slice: x: 4, y: 8, z: 8, core: 2. Of those that a mesh axis runs over, the one named last changes fastest.
Arguments:
- tokens: bfloat16 [65536, 3584], P(('dp', 'expert')), may hold values from -6 to 6
- cotangent: bfloat16 [65536, 3584], P(('dp', 'expert')), may hold values from -6 to 6
- route_ids: int32 [65536, 8], P(('dp', 'expert')), may hold values from 0 to 255, as said below
- route_gates: float32 [65536, 8], P(('dp', 'expert')), may hold values from 0.1 to 1
- gate_w: bfloat16 [3584, 8192], P('dp', 'expert'), may hold values from -0.09375 to 0.09375
- up_w: bfloat16 [3584, 8192], P('dp', 'expert'), may hold values from -0.09375 to 0.09375
- down_w: bfloat16 [3584, 8192], P('dp', 'expert'), may hold values from -0.1875 to 0.1875
Outputs:
- moe_out: bfloat16 [65536, 3584], P(('dp', 'expert'))
- d_tokens: bfloat16 [65536, 3584], P(('dp', 'expert'))
- d_gates: float32 [65536, 8], P(('dp', 'expert'))
- d_gate_w: bfloat16 [3584, 8192], P('dp', 'expert')
- d_up_w: bfloat16 [3584, 8192], P('dp', 'expert')
- d_down_w: bfloat16 [3584, 8192], P('dp', 'expert')
Inputs may be any that keep to these rules, and one draw needn't show every extreme that they name: `route_ids`: each token names 8 different experts; the experts in flight are 0 to 7. Among the tokens of one device (aligned blocks of 128 tokens) each expert in flight is named by at most 6 tokens, and in every draw one expert in flight is named by exactly 6 tokens in every block.
All inputs are finite; a program needn't handle non-finite values.
Results may differ from a plain program's by a relative error of at most 0.017.
Values may be sent and summed in bfloat16 or wider, within the bound.
A program may use at most 64 MiB of HBM per device.

v0:
```python
import jax
import jax.numpy as jnp
from jax import lax
from jax.sharding import Mesh, PartitionSpec as P

SLICES = 8
CAP = 6
PAD = 8
BF = jnp.bfloat16
F32 = jnp.float32
CONTRACT_COLS = (((1,), (1,)), ((), ()))
CONTRACT_ROWS = (((0,), (0,)), ((), ()))


def dot(a, b, dims=(((1,), (0,)), ((), ()))):
    return lax.dot_general(a, b, dims, preferred_element_type=F32)


def routing(route_ids, route_gates, groups):
    tok_rows = route_ids.shape[0]
    experts = jnp.arange(groups, dtype=jnp.int32)
    match = route_ids[:, :, None] == experts[None, None, :]
    member = jnp.sum(match.astype(F32), axis=1)
    gate = jnp.sum(jnp.where(match, route_gates[:, :, None], 0.0), axis=1)
    row = lax.broadcasted_iota(jnp.int32, (tok_rows, tok_rows), 0)
    col = lax.broadcasted_iota(jnp.int32, (tok_rows, tok_rows), 1)
    before = (col < row).astype(BF)
    slot = dot(before, member.astype(BF))
    return (match, member, gate, slot)


def shards(tokens, cotangent, route_ids, route_gates, gate_w, up_w, down_w):
    groups = lax.axis_size("y")
    width = tokens.shape[1]
    tok_rows = tokens.shape[0]
    hid = gate_w.shape[1]
    match, member, gate, slot = routing(route_ids, route_gates, groups)
    wide = jnp.where(member > 0.5, slot, -1.0).T[:, None, :]
    sel = (wide == jnp.arange(PAD, dtype=F32)[None, :, None]).astype(F32)
    gates_t = gate.T[:, None, :]
    slot_gate = jnp.sum(sel * gates_t, axis=2)
    pick = sel.reshape(groups * PAD, tok_rows).astype(BF)
    token_slots = dot(pick, tokens).astype(BF)
    cot_slots = dot(pick, cotangent)
    scaled_slots = (slot_gate.reshape(groups * PAD, 1) * cot_slots).astype(BF)
    send = jnp.concatenate(
        [token_slots.reshape(groups, PAD, width), scaled_slots.reshape(groups, PAD, width)], axis=1
    )
    w_all = lax.all_gather(
        jnp.concatenate([gate_w, up_w, down_w], axis=1), "dp", axis=0, tiled=True
    )
    w_gate, w_up, w_down = (w_all[:, :hid], w_all[:, hid : 2 * hid], w_all[:, 2 * hid :])
    came = lax.all_to_all(send, "y", split_axis=0, concat_axis=0, tiled=True)
    rows = groups * CAP
    out_row = lax.broadcasted_iota(jnp.int32, (2 * rows, groups * 2 * PAD), 0)
    in_row = lax.broadcasted_iota(jnp.int32, (2 * rows, groups * 2 * PAD), 1)
    kind = (out_row >= rows).astype(jnp.int32)
    local = out_row - kind * rows
    wanted = local // CAP * (2 * PAD) + kind * PAD + local % CAP
    squeeze = (in_row == wanted).astype(BF)
    compact = dot(squeeze, came.reshape(groups * 2 * PAD, width)).astype(BF)
    both = lax.all_gather(compact, ("x", "c"), axis=0, tiled=False)
    n_slices = both.shape[0]
    token_rows = both[:, :rows].reshape(n_slices * rows, width)
    scaled_rows = both[:, rows:].reshape(n_slices * rows, width)
    gate_pre = dot(token_rows, w_gate)
    up_pre = dot(token_rows, w_up)
    sig = jax.nn.sigmoid(gate_pre)
    active = gate_pre * sig
    hidden = (active * up_pre).astype(BF)
    d_hidden = dot(scaled_rows, w_down)
    d_gate_pre = (d_hidden * up_pre * sig * (1.0 + gate_pre * (1.0 - sig))).astype(BF)
    d_up_pre = (d_hidden * active).astype(BF)
    out_part = dot(hidden, w_down, CONTRACT_COLS).astype(BF)
    dx_part = (dot(d_gate_pre, w_gate, CONTRACT_COLS) + dot(d_up_pre, w_up, CONTRACT_COLS)).astype(
        BF
    )
    parts = jnp.concatenate(
        [out_part.reshape(n_slices, rows, width), dx_part.reshape(n_slices, rows, width)], axis=1
    ).reshape(n_slices * 2 * rows, width)
    summed = lax.psum_scatter(parts, ("x", "c"), scatter_dimension=0, tiled=True)
    grads = jnp.concatenate(
        [
            dot(token_rows, d_gate_pre, CONTRACT_ROWS),
            dot(token_rows, d_up_pre, CONTRACT_ROWS),
            dot(scaled_rows, hidden, CONTRACT_ROWS),
        ],
        axis=1,
    ).astype(BF)
    grads = lax.psum_scatter(grads, "dp", scatter_dimension=0, tiled=True)
    back = dot(squeeze, summed, CONTRACT_ROWS).astype(BF).reshape(groups, 2 * PAD, width)
    back = lax.all_to_all(back, "y", split_axis=0, concat_axis=0, tiled=True)
    back = back.reshape(groups * 2 * PAD, width)
    zero = jnp.zeros_like(sel)
    member_out = jnp.concatenate([sel, zero], axis=1).reshape(groups * 2 * PAD, tok_rows)
    member_dx = jnp.concatenate([zero, sel], axis=1).reshape(groups * 2 * PAD, tok_rows)
    weight = jnp.concatenate([sel * gates_t, zero], axis=1).reshape(groups * 2 * PAD, tok_rows)
    high = weight.astype(BF)
    low = (weight - high.astype(F32)).astype(BF)
    moe_out = (dot(high, back, CONTRACT_ROWS) + dot(low, back, CONTRACT_ROWS)).astype(BF)
    d_tokens = dot(member_dx.astype(BF), back, CONTRACT_ROWS).astype(BF)
    inner = dot(back, cotangent, CONTRACT_COLS) * member_out
    by_expert = jnp.sum(inner.reshape(groups, 2 * PAD, tok_rows), axis=1).T
    d_gates = jnp.sum(jnp.where(match, by_expert[:, None, :], 0.0), axis=2)
    return (
        moe_out,
        d_tokens,
        d_gates,
        grads[:, :hid],
        grads[:, hid : 2 * hid],
        grads[:, 2 * hid :],
    )


def solution(mesh):
    dp, owners = mesh.devices.shape
    y = owners // SLICES
    grid = Mesh(mesh.devices.reshape(dp, y, SLICES // 2, 2), ("dp", "y", "x", "c"))
    rows = P(("dp", "y", "x", "c"), None)
    cols = P("dp", ("y", "x", "c"))
    return jax.shard_map(
        shards,
        mesh=grid,
        in_specs=(rows, rows, rows, rows, cols, cols, cols),
        out_specs=(rows, rows, rows, cols, cols, cols),
        check_vma=False,
    )
```

profile of v0, /device:TPU:2, one launch (start us, length us, event | category | flops | bytes accessed | tf_op | source)
XLA Modules:
  0.0 255.6 jit_solution(2671036714309216586)
XLA Ops:
  8.4 1.5 fusion.6
  10.3 1.0 pad_maximum_fusion.2
  11.3 7.1 %all-to-all-start = ((bf16[8,16,3584]{2,1,0:T(8,128)(2,1)}), bf16[8,16,3584]{2,1,0:T(8,128)(2,1)S(1)}, u32[]{:S(2)}, u32[]{:S(2)}) async-start(bf16[8,16,3584]{2,1,0:T(8,128)(2,1)} %pad_maximum_fusion.2), calls=%async_computation | async-start | bytes 1835008 | tf_op jit(solution)/shard_map/all_to_all | solution.py:53
  18.5 25.8 %all-to-all-done = bf16[8,16,3584]{2,1,0:T(8,128)(2,1)S(1)} async-done(((bf16[8,16,3584]{2,1,0:T(8,128)(2,1)}), bf16[8,16,3584]{2,1,0:T(8,128)(2,1)S(1)}, u32[]{:S(2)}, u32[]{:S(2)}) %all-to-all-start) | async-done | bytes 917536 | tf_op jit(solution)/shard_map/all_to_all | solution.py:53
  44.3 1.3 convolution_convert_fusion.5
  46.5 40.6 %all-gather.6.cloned.1.call-done = bf16[768,3584]{1,0:T(8,128)(2,1)} async-done(((bf16[96,3584]{1,0:T(8,128)(2,1)}), bf16[768,3584]{1,0:T(8,128)(2,1)}) %all-gather.6.cloned.1.call-update) | async-done | bytes 5505040 | tf_op jit(solution)/shard_map/all_gather | solution.py:62
  87.2 5.5 %fusion.33 = (bf16[8,48,3584]{2,1,0:T(8,128)(2,1)}, bf16[8,48,3584]{2,1,0:T(8,128)(2,1)}) fusion(bf16[8,96,3584]{2,1,0:T(8,128)(2,1)} %bitcast.70), kind=kLoop, calls=%fused_computation.75 | loop fusion | bytes 11010048 | tf_op jit(solution)/shard_map/slice | solution.py:65
  92.6 44.5 %all-gather.4.cloned.1.call-done = bf16[3584,384]{1,0:T(8,128)(2,1)} async-done(((bf16[448,384]{1,0:T(8,128)(2,1)}), bf16[3584,384]{1,0:T(8,128)(2,1)}) %all-gather.4.cloned.1.call-update) | async-done | bytes 2752528 | tf_op jit(solution)/shard_map/all_gather | solution.py:49
  137.1 3.0 %fusion.15 = f32[384,128]{1,0:T(8,128)S(1)} fusion(bf16[384,3584]{1,0:T(8,128)(2,1)} %bitcast.60, bf16[3584,384]{1,0:T(8,128)(2,1)} %all-gather.4.cloned.1.call-done), kind=kOutput, calls=%fused_computation.32 | convolution fusion | flops 352321536 | bytes 3866624 | tf_op jit(solution)/shard_map/dot_general | solution.py:16
  140.2 2.2 fusion.7
  142.4 0.9 multiply_convert_fusion.2
  144.2 0.9 convolution_convert_fusion
  145.0 0.9 fusion
  145.9 2.8 %pad_maximum_fusion = bf16[8,96,3584]{2,1,0:T(8,128)(2,1)} fusion(bf16[8,48,3584]{2,1,0:T(8,128)(2,1)S(1)} %bitcast.69, bf16[8,48,3584]{2,1,0:T(8,128)(2,1)S(1)} %bitcast.68), kind=kLoop, calls=%fused_computation.3 | loop fusion | flops 11010048 | bytes 11010048 | tf_op jit(solution)/shard_map/concatenate | solution.py:78
  148.8 2.6 %convolution_convert_fusion.1 = bf16[3584,128]{0,1:T(8,128)(2,1)S(1)} fusion(bf16[384,3584]{1,0:T(8,128)(2,1)} %bitcast.66, bf16[384,128]{1,0:T(8,128)(2,1)S(1)} %get-tuple-element.28), kind=kOutput, calls=%fused_computation.10 | convolution fusion | flops 352780288 | bytes 3768320 | tf_op jit(solution)/shard_map/dot_general | solution.py:16
  152.8 1.8 pad_maximum_fusion.1
  154.6 4.5 %copy.27 = bf16[3584,384]{1,0:T(8,128)(2,1)} copy(bf16[3584,384]{0,1:T(8,128)(2,1)} %pad_maximum_fusion.1) | data formatting | bytes 5505024
  159.2 30.2 %reduce-scatter.5.cloned.1.call-done = bf16[96,3584]{1,0:T(8,128)(2,1)} async-done(((bf16[768,3584]{1,0:T(8,128)(2,1)}), bf16[96,3584]{1,0:T(8,128)(2,1)}) %reduce-scatter.5.cloned.1.call-update) | async-done | bytes 688144 | tf_op jit(solution)/shard_map/reduce_scatter | solution.py:81
  189.3 2.6 %convolution_convert_fusion.4 = bf16[128,3584]{1,0:T(8,128)(2,1)} fusion(bf16[96,3584]{1,0:T(8,128)(2,1)} %reduce-scatter.5.cloned.1.call-done, s32[96]{0:T(128)S(1)} %broadcast_remainder_fusion, s32[96]{0:T(128)S(1)} %get-tuple-element.42, s32[96]{0:T(128)S(1)} %get-tuple-element.40, s32[96]{0:T(128)S(1)} %get-tuple-element.43, ...), kind=kOutput, calls=%fused_computation.13 | convolution fusion | flops 88612864 | bytes 1607744 | tf_op jit(solution)/shard_map/dot_general | solution.py:16
  191.9 6.8 %all-to-all-start.1 = ((bf16[8,16,3584]{2,1,0:T(8,128)(2,1)}), bf16[8,16,3584]{2,1,0:T(8,128)(2,1)S(1)}, u32[]{:S(2)}, u32[]{:S(2)}) async-start(bf16[8,16,3584]{2,1,0:T(8,128)(2,1)} %bitcast.12), calls=%async_computation.2 | async-start | bytes 1835008 | tf_op jit(solution)/shard_map/all_to_all | solution.py:92
  198.8 44.4 %reduce-scatter.7.cloned.1.call-done = bf16[448,384]{1,0:T(8,128)(2,1)} async-done(((bf16[3584,384]{1,0:T(8,128)(2,1)}), bf16[448,384]{1,0:T(8,128)(2,1)}) %reduce-scatter.7.cloned.1.call-update) | async-done | bytes 344080
  243.2 1.7 fusion.34
  246.4 1.4 fusion.2
  247.8 1.3 fusion.3
  (47 shorter events, 6.4 us)
Async XLA Ops:
  7.2 2.8 %copy-start = (bf16[128,3584]{1,0:T(8,128)(2,1)S(1)}, bf16[128,3584]{1,0:T(8,128)(2,1)}, u32[]{:S(2)}) copy-start(bf16[128,3584]{1,0:T(8,128)(2,1)} %param.8) | copy-start | bytes 2752516
  10.3 35.4 %copy-start.5 = (bf16[448,128]{1,0:T(8,128)(2,1)S(1)}, bf16[448,128]{1,0:T(8,128)(2,1)}, u32[]{:S(2)}) copy-start(bf16[448,128]{1,0:T(8,128)(2,1)} %param.13) | copy-start | bytes 344068
  10.3 35.4 %copy-start.6 = (bf16[448,128]{1,0:T(8,128)(2,1)S(1)}, bf16[448,128]{1,0:T(8,128)(2,1)}, u32[]{:S(2)}) copy-start(bf16[448,128]{1,0:T(8,128)(2,1)} %param.12) | copy-start | bytes 344068
  10.3 35.4 %copy-start.7 = (bf16[448,128]{1,0:T(8,128)(2,1)S(1)}, bf16[448,128]{1,0:T(8,128)(2,1)}, u32[]{:S(2)}) copy-start(bf16[448,128]{1,0:T(8,128)(2,1)} %param.11) | copy-start | bytes 344068
  11.3 33.0 %all-to-all-start = ((bf16[8,16,3584]{2,1,0:T(8,128)(2,1)}), bf16[8,16,3584]{2,1,0:T(8,128)(2,1)S(1)}, u32[]{:S(2)}, u32[]{:S(2)}) async-start(bf16[8,16,3584]{2,1,0:T(8,128)(2,1)} %pad_maximum_fusion.2), calls=%async_computation | async-start | bytes 1835008 | tf_op jit(solution)/shard_map/all_to_all | solution.py:53
  18.4 68.8 %all-gather.6.cloned.1.call-start = ((), (), s32[]{:S(2)}) async-start(), calls=%async_computation.6 | async-start | bytes 6193152 | tf_op jit(solution)/shard_map/all_gather | solution.py:62
  45.6 91.5 %all-gather.4.cloned.1.call-start = ((), (), s32[]{:S(2)}) async-start(), calls=%async_computation.4 | async-start | bytes 3096576 | tf_op jit(solution)/shard_map/all_gather | solution.py:49
  46.5 142.8 %reduce-scatter.5.cloned.1.call-start = ((), (), s32[]{:S(2)}) async-start(), calls=%async_computation.5 | async-start | bytes 6193152 | tf_op jit(solution)/shard_map/reduce_scatter | solution.py:81
  137.1 3.0 %copy-start.3 = (bf16[8,48,3584]{2,1,0:T(8,128)(2,1)S(1)}, bf16[8,48,3584]{2,1,0:T(8,128)(2,1)}, u32[]{:S(2)}) copy-start(bf16[8,48,3584]{2,1,0:T(8,128)(2,1)} %get-tuple-element.26) | copy-start | bytes 8257540
  137.1 5.3 %copy-start.4 = (bf16[3584,384]{1,0:T(8,128)(2,1)S(1)}, bf16[3584,384]{1,0:T(8,128)(2,1)}, u32[]{:S(2)}) copy-start(bf16[3584,384]{1,0:T(8,128)(2,1)} %all-gather.4.cloned.1.call-done) | copy-start | bytes 8257540
  140.2 2.2 copy-start.1
  148.7 94.5 %reduce-scatter.7.cloned.1.call-start = ((), (), s32[]{:S(2)}) async-start(), calls=%async_computation.7 | async-start | bytes 3096576
  148.8 2.6 %copy-start.2 = (bf16[8,48,3584]{2,1,0:T(8,128)(2,1)S(1)}, bf16[8,48,3584]{2,1,0:T(8,128)(2,1)}, u32[]{:S(2)}) copy-start(bf16[8,48,3584]{2,1,0:T(8,128)(2,1)} %get-tuple-element.27) | copy-start | bytes 8257540
  159.2 86.2 %copy-start.8 = (s32[128,8]{0,1:T(8,128)S(1)}, s32[128,8]{0,1:T(8,128)}, u32[]{:S(2)}) copy-start(s32[128,8]{0,1:T(8,128)} %param.9) | copy-start | bytes 12292
  191.9 53.0 %all-to-all-start.1 = ((bf16[8,16,3584]{2,1,0:T(8,128)(2,1)}), bf16[8,16,3584]{2,1,0:T(8,128)(2,1)S(1)}, u32[]{:S(2)}, u32[]{:S(2)}) async-start(bf16[8,16,3584]{2,1,0:T(8,128)(2,1)} %bitcast.12), calls=%async_computation.2 | async-start | bytes 1835008 | tf_op jit(solution)/shard_map/all_to_all | solution.py:92
Sparse Core Ops, SparseCore 0:
  45.7 41.3 all-gather.5
  89.8 47.2 all-gather.3
  148.8 40.4 reduce-scatter.4
  192.0 51.1 reduce-scatter.6
where the time goes:
time: 256 us
  waiting for transfers between devices  186 us (73%)
  matrix products  22.1 us (9%)
  starting transfers between devices  14.1 us (6%)
  between operations  14 us (5%)
  local copies, waits for them, and re-layouts  12 us (5%)
  other arithmetic  7.87 us (3%)
    unnamed x5, waiting for transfers between devices  44.5 us
    all_gather x1, waiting for transfers between devices, shards(): lax.all_gather(jnp.concatenate([gate_w, up_w, down_w], axis=1), 'dp', axi...  44.5 us
    all_gather x1, waiting for transfers between devices, shards(): both = lax.all_gather(compact, ('x', 'c'), axis=0, tiled=False)  40.6 us
    reduce_scatter x1, waiting for transfers between devices, shards(): lax.psum_scatter(parts, ('x', 'c'), scatter_dimension=0, tiled=True)  30.2 us
    all_to_all x1, waiting for transfers between devices, shards(): came = lax.all_to_all(send, 'y', split_axis=0, concat_axis=0, tiled=True)  25.8 us
    dot_general x18, matrix products, dot(): return lax.dot_general(a, b, dims, preferred_element_type=F32)  22.1 us
    all_to_all x1, starting transfers between devices, shards(): came = lax.all_to_all(send, 'y', split_axis=0, concat_axis=0, tiled=True)  7.09 us
    all_to_all x1, starting transfers between devices, shards(): back = lax.all_to_all(back, 'y', split_axis=0, concat_axis=0, tiled=True)  6.82 us
  transfers between devices with their start and end apart: 6, of which 5 were waited for; matrix products, arithmetic and copies ran while one was open for 8% of the time, Pallas kernels for 0%

commit v1 on v0

--- a/solution.py
+++ b/solution.py
@@ -10,6 +10,24 @@
 F32 = jnp.float32
 CONTRACT_COLS = (((1,), (1,)), ((), ()))
 CONTRACT_ROWS = (((0,), (0,)), ((), ()))
+
+
+def gather_around(shard, axis, dim):
+    ways, here, step = (lax.axis_size(axis), lax.axis_index(axis), shard.shape[dim])
+    shape = [n * ways if d == dim else n for d, n in enumerate(shard.shape)]
+    full = lax.dynamic_update_slice_in_dim(
+        jnp.zeros(shape, shard.dtype), shard, here * step, axis=dim
+    )
+    going_up = going_down = shard
+    for far in range(1, ways // 2 + 1):
+        going_up = lax.ppermute(going_up, axis, [(d, (d + 1) % ways) for d in range(ways)])
+        full = lax.dynamic_update_slice_in_dim(full, going_up, (here - far) % ways * step, axis=dim)
+        if 2 * far < ways:
+            going_down = lax.ppermute(going_down, axis, [(d, (d - 1) % ways) for d in range(ways)])
+            full = lax.dynamic_update_slice_in_dim(
+                full, going_down, (here + far) % ways * step, axis=dim
+            )
+    return full
 
 
 def dot(a, b, dims=(((1,), (0,)), ((), ()))):
@@ -46,9 +64,7 @@
     send = jnp.concatenate(
         [token_slots.reshape(groups, PAD, width), scaled_slots.reshape(groups, PAD, width)], axis=1
     )
-    w_all = lax.all_gather(
-        jnp.concatenate([gate_w, up_w, down_w], axis=1), "dp", axis=0, tiled=True
-    )
+    w_all = gather_around(jnp.concatenate([gate_w, up_w, down_w], axis=1), "dp", 0)
     w_gate, w_up, w_down = (w_all[:, :hid], w_all[:, hid : 2 * hid], w_all[:, 2 * hid :])
     came = lax.all_to_all(send, "y", split_axis=0, concat_axis=0, tiled=True)
     rows = groups * CAP

time: 256 us -> 222 us (0.87)
  the two profiles are of different devices: /device:TPU:2 before, /device:TPU:10 now
where the time goes in v1:
time: 222 us; the launch traced here: 221 us
  waiting for transfers between devices  112 us (50%)
  starting transfers between devices  44 us (20%)
  matrix products  26.5 us (12%)
  local copies, waits for them, and re-layouts  17.5 us (8%)
  between operations  14.2 us (6%)
  other arithmetic  7.02 us (3%)
    unnamed x4, waiting for transfers between devices  44.3 us
    reduce_scatter x1, waiting for transfers between devices, shards(): lax.psum_scatter(parts, ('x', 'c'), scatter_dimension=0, tiled=True)  31.9 us
    dot_general x18, matrix products, dot(): return lax.dot_general(a, b, dims, preferred_element_type=F32)  26.5 us
    all_to_all x1, waiting for transfers between devices, shards(): came = lax.all_to_all(send, 'y', split_axis=0, concat_axis=0, tiled=True)  24.4 us
    ppermute x3, starting transfers between devices, gather_around(): lax.ppermute(going_down, axis, [(d, (d - 1) % ways) for d in range(ways)])  18.9 us
    ppermute x4, waiting for transfers between devices, gather_around(): lax.ppermute(going_up, axis, [(d, (d + 1) % ways) for d in range(ways)])  11.4 us
    ppermute x4, starting transfers between devices, gather_around(): lax.ppermute(going_up, axis, [(d, (d + 1) % ways) for d in range(ways)])  10 us
    all_to_all x1, starting transfers between devices, shards(): came = lax.all_to_all(send, 'y', split_axis=0, concat_axis=0, tiled=True)  7.68 us
  transfers between devices with their start and end apart: 12, of which 7 were waited for; matrix products, arithmetic and copies ran while one was open for 10% of the time, Pallas kernels for 0%

profile of v1, /device:TPU:10, one launch (start us, length us, event | category | flops | bytes accessed | tf_op | source)
XLA Modules:
  0.0 221.2 jit_solution(16458480490275799446)
XLA Ops:
  11.3 7.7 %all-to-all-start = ((bf16[8,16,3584]{2,1,0:T(8,128)(2,1)}), bf16[8,16,3584]{2,1,0:T(8,128)(2,1)S(1)}, u32[]{:S(2)}, u32[]{:S(2)}) async-start(bf16[8,16,3584]{2,1,0:T(8,128)(2,1)} %pad_maximum_fusion.2), calls=%async_computation | async-start | bytes 1835008 | tf_op jit(solution)/shard_map/all_to_all | solution.py:69
  19.0 24.4 %all-to-all-done = bf16[8,16,3584]{2,1,0:T(8,128)(2,1)S(1)} async-done(((bf16[8,16,3584]{2,1,0:T(8,128)(2,1)}), bf16[8,16,3584]{2,1,0:T(8,128)(2,1)S(1)}, u32[]{:S(2)}, u32[]{:S(2)}) %all-to-all-start) | async-done | bytes 917536 | tf_op jit(solution)/shard_map/all_to_all | solution.py:69
  44.9 4.3 %collective-permute-start = (bf16[448,384]{1,0:T(8,128)(2,1)S(1)}, bf16[448,384]{1,0:T(8,128)(2,1)S(1)}, u32[]{:S(2)}, u32[]{:S(2)}) collective-permute-start(bf16[448,384]{1,0:T(8,128)(2,1)S(1)} %constant_dynamic-update-slice_fusion), channel_id=1, source_target_pairs={{0,64},{64,128},{128,192},{192,256},{256,320},{320,384},{384,448},... | collective-permute-start | bytes 1032200 | tf_op jit(solution)/shard_map/ppermute | solution.py:23
  49.2 8.6 %collective-permute-start.1 = (bf16[448,384]{1,0:T(8,128)(2,1)S(1)}, bf16[448,384]{1,0:T(8,128)(2,1)S(1)}, u32[]{:S(2)}, u32[]{:S(2)}) collective-permute-start(bf16[448,384]{1,0:T(8,128)(2,1)S(1)} %constant_dynamic-update-slice_fusion), channel_id=1, source_target_pairs={{0,448},{64,0},{128,64},{192,128},{256,192},{320,256},{384,320},{4... | collective-permute-start | bytes 1032200 | tf_op jit(solution)/shard_map/ppermute | solution.py:26
  57.8 3.7 %collective-permute-done = bf16[448,384]{1,0:T(8,128)(2,1)S(1)} collective-permute-done((bf16[448,384]{1,0:T(8,128)(2,1)S(1)}, bf16[448,384]{1,0:T(8,128)(2,1)S(1)}, u32[]{:S(2)}, u32[]{:S(2)}) %collective-permute-start) | collective-permute-done | bytes 344096 | tf_op jit(solution)/shard_map/ppermute | solution.py:23
  61.5 1.9 collective-permute-start.2
  63.6 5.1 %collective-permute-start.3 = (bf16[448,384]{1,0:T(8,128)(2,1)S(1)}, bf16[448,384]{1,0:T(8,128)(2,1)S(1)}, u32[]{:S(2)}, u32[]{:S(2)}) collective-permute-start(bf16[448,384]{1,0:T(8,128)(2,1)S(1)} %collective-permute-done.1), channel_id=1, source_target_pairs={{0,448},{64,0},{128,64},{192,128},{256,192},{320,256},{384,320},{4... | collective-permute-start | bytes 1032200 | tf_op jit(solution)/shard_map/ppermute | solution.py:26
  71.8 1.9 collective-permute-start.4
  75.3 5.1 %collective-permute-start.5 = (bf16[448,384]{1,0:T(8,128)(2,1)S(1)}, bf16[448,384]{1,0:T(8,128)(2,1)S(1)}, u32[]{:S(2)}, u32[]{:S(2)}) collective-permute-start(bf16[448,384]{1,0:T(8,128)(2,1)S(1)} %collective-permute-done.3), channel_id=1, source_target_pairs={{0,448},{64,0},{128,64},{192,128},{256,192},{320,256},{384,320},{4... | collective-permute-start | bytes 1032200 | tf_op jit(solution)/shard_map/ppermute | solution.py:26
  86.5 6.1 %collective-permute-done.6 = bf16[448,384]{1,0:T(8,128)(2,1)S(1)} collective-permute-done((bf16[448,384]{1,0:T(8,128)(2,1)S(1)}, bf16[448,384]{1,0:T(8,128)(2,1)S(1)}, u32[]{:S(2)}, u32[]{:S(2)}) %collective-permute-start.6) | collective-permute-done | bytes 344096 | tf_op jit(solution)/shard_map/ppermute | solution.py:23
  93.3 3.0 %fusion.33 = (bf16[8,48,3584]{2,1,0:T(8,128)(2,1)S(1)}, bf16[8,48,3584]{2,1,0:T(8,128)(2,1)S(1)}) fusion(bf16[8,96,3584]{2,1,0:T(8,128)(2,1)} %bitcast.70), kind=kLoop, calls=%fused_computation.85 | loop fusion | bytes 11010048 | tf_op jit(solution)/shard_map/slice | solution.py:80
  96.3 2.8 %fusion.7 = f32[384,128]{1,0:T(8,128)S(1)} fusion(bf16[384,3584]{1,0:T(8,128)(2,1)S(1)} %bitcast.66, bf16[3584,384]{1,0:T(8,128)(2,1)} %constant_dynamic-update-slice_fusion.3), kind=kOutput, calls=%fused_computation.24 | convolution fusion | flops 352321536 | bytes 3866624 | tf_op jit(solution)/shard_map/dot_general | solution.py:34
  99.0 2.1 fusion.15
  101.1 2.1 multiply_convert_fusion.2
  103.2 2.1 convolution_convert_fusion
  105.3 2.1 fusion.10
  107.3 2.1 fusion
  109.4 2.8 %pad_maximum_fusion = bf16[8,96,3584]{2,1,0:T(8,128)(2,1)} fusion(bf16[8,48,3584]{2,1,0:T(8,128)(2,1)S(1)} %bitcast.69, bf16[8,48,3584]{2,1,0:T(8,128)(2,1)S(1)} %bitcast.68), kind=kLoop, calls=%fused_computation.3 | loop fusion | flops 11010048 | bytes 11010048 | tf_op jit(solution)/shard_map/concatenate | solution.py:94
  112.3 2.6 %convolution_convert_fusion.1 = bf16[3584,128]{0,1:T(8,128)(2,1)S(1)} fusion(bf16[384,3584]{1,0:T(8,128)(2,1)} %bitcast.67, bf16[384,128]{1,0:T(8,128)(2,1)S(1)} %get-tuple-element.28), kind=kOutput, calls=%fused_computation.10 | convolution fusion | flops 352780288 | bytes 3768320 | tf_op jit(solution)/shard_map/dot_general | solution.py:34
  118.0 4.5 %copy.27 = bf16[3584,384]{1,0:T(8,128)(2,1)} copy(bf16[3584,384]{0,1:T(8,128)(2,1)} %pad_maximum_fusion.1) | data formatting | bytes 5505024
  122.6 31.9 %reduce-scatter.5.cloned.1.call-done = bf16[96,3584]{1,0:T(8,128)(2,1)} async-done(((bf16[768,3584]{1,0:T(8,128)(2,1)}), bf16[96,3584]{1,0:T(8,128)(2,1)}) %reduce-scatter.5.cloned.1.call-update) | async-done | bytes 688144 | tf_op jit(solution)/shard_map/reduce_scatter | solution.py:97
  154.5 2.6 %convolution_convert_fusion.4 = bf16[128,3584]{1,0:T(8,128)(2,1)} fusion(bf16[96,3584]{1,0:T(8,128)(2,1)} %reduce-scatter.5.cloned.1.call-done, s32[96]{0:T(128)S(1)} %broadcast_remainder_fusion, s32[96]{0:T(128)S(1)} %get-tuple-element.42, s32[96]{0:T(128)S(1)} %get-tuple-element.40, s32[96]{0:T(128)S(1)} %get-tuple-element.43, ...), kind=kOutput, calls=%fused_computation.13 | convolution fusion | flops 88612864 | bytes 1607744 | tf_op jit(solution)/shard_map/dot_general | solution.py:34
  157.1 7.4 %all-to-all-start.1 = ((bf16[8,16,3584]{2,1,0:T(8,128)(2,1)}), bf16[8,16,3584]{2,1,0:T(8,128)(2,1)S(1)}, u32[]{:S(2)}, u32[]{:S(2)}) async-start(bf16[8,16,3584]{2,1,0:T(8,128)(2,1)} %bitcast.12), calls=%async_computation.2 | async-start | bytes 1835008 | tf_op jit(solution)/shard_map/all_to_all | solution.py:108
  164.5 44.2 %reduce-scatter.7.cloned.1.call-done = bf16[448,384]{1,0:T(8,128)(2,1)} async-done(((bf16[3584,384]{1,0:T(8,128)(2,1)}), bf16[448,384]{1,0:T(8,128)(2,1)}) %reduce-scatter.7.cloned.1.call-update) | async-done | bytes 344080
  (67 shorter events, 26.1 us)
Async XLA Ops:
  7.2 2.7 %copy-start = (bf16[128,3584]{1,0:T(8,128)(2,1)S(1)}, bf16[128,3584]{1,0:T(8,128)(2,1)}, u32[]{:S(2)}) copy-start(bf16[128,3584]{1,0:T(8,128)(2,1)} %param.8) | copy-start | bytes 2752516
  10.3 34.5 %copy-start.4 = (bf16[448,128]{1,0:T(8,128)(2,1)S(1)}, bf16[448,128]{1,0:T(8,128)(2,1)}, u32[]{:S(2)}) copy-start(bf16[448,128]{1,0:T(8,128)(2,1)} %param.11) | copy-start | bytes 344068
  10.3 34.5 %copy-start.5 = (bf16[448,128]{1,0:T(8,128)(2,1)S(1)}, bf16[448,128]{1,0:T(8,128)(2,1)}, u32[]{:S(2)}) copy-start(bf16[448,128]{1,0:T(8,128)(2,1)} %param.12) | copy-start | bytes 344068
  11.3 33.6 %copy-start.6 = (bf16[448,128]{1,0:T(8,128)(2,1)S(1)}, bf16[448,128]{1,0:T(8,128)(2,1)}, u32[]{:S(2)}) copy-start(bf16[448,128]{1,0:T(8,128)(2,1)} %param.13) | copy-start | bytes 344068
  11.3 32.1 %all-to-all-start = ((bf16[8,16,3584]{2,1,0:T(8,128)(2,1)}), bf16[8,16,3584]{2,1,0:T(8,128)(2,1)S(1)}, u32[]{:S(2)}, u32[]{:S(2)}) async-start(bf16[8,16,3584]{2,1,0:T(8,128)(2,1)} %pad_maximum_fusion.2), calls=%async_computation | async-start | bytes 1835008 | tf_op jit(solution)/shard_map/all_to_all | solution.py:69
  18.9 74.3 %all-gather.3.cloned.1.call-start = ((), (), s32[]{:S(2)}) async-start(), calls=%async_computation.5 | async-start | bytes 6193152 | tf_op jit(solution)/shard_map/all_gather | solution.py:78
  44.7 109.8 %reduce-scatter.5.cloned.1.call-start = ((), (), s32[]{:S(2)}) async-start(), calls=%async_computation.4 | async-start | bytes 6193152 | tf_op jit(solution)/shard_map/reduce_scatter | solution.py:97
  44.9 16.6 %collective-permute-start = (bf16[448,384]{1,0:T(8,128)(2,1)S(1)}, bf16[448,384]{1,0:T(8,128)(2,1)S(1)}, u32[]{:S(2)}, u32[]{:S(2)}) collective-permute-start(bf16[448,384]{1,0:T(8,128)(2,1)S(1)} %constant_dynamic-update-slice_fusion), channel_id=1, source_target_pairs={{0,64},{64,128},{128,192},{192,256},{256,320},{320,384},{384,448},... | collective-permute-start | bytes 1032200 | tf_op jit(solution)/shard_map/ppermute | solution.py:23
  49.2 14.4 %collective-permute-start.1 = (bf16[448,384]{1,0:T(8,128)(2,1)S(1)}, bf16[448,384]{1,0:T(8,128)(2,1)S(1)}, u32[]{:S(2)}, u32[]{:S(2)}) collective-permute-start(bf16[448,384]{1,0:T(8,128)(2,1)S(1)} %constant_dynamic-update-slice_fusion), channel_id=1, source_target_pairs={{0,448},{64,0},{128,64},{192,128},{256,192},{320,256},{384,320},{4... | collective-permute-start | bytes 1032200 | tf_op jit(solution)/shard_map/ppermute | solution.py:26
  61.5 10.3 %collective-permute-start.2 = (bf16[448,384]{1,0:T(8,128)(2,1)S(1)}, bf16[448,384]{1,0:T(8,128)(2,1)S(1)}, u32[]{:S(2)}, u32[]{:S(2)}) collective-permute-start(bf16[448,384]{1,0:T(8,128)(2,1)S(1)} %collective-permute-done), channel_id=1, source_target_pairs={{0,64},{64,128},{128,192},{192,256},{256,320},{320,384},{384,448},... | collective-permute-start | bytes 1032200 | tf_op jit(solution)/shard_map/ppermute | solution.py:23
  63.6 11.7 %collective-permute-start.3 = (bf16[448,384]{1,0:T(8,128)(2,1)S(1)}, bf16[448,384]{1,0:T(8,128)(2,1)S(1)}, u32[]{:S(2)}, u32[]{:S(2)}) collective-permute-start(bf16[448,384]{1,0:T(8,128)(2,1)S(1)} %collective-permute-done.1), channel_id=1, source_target_pairs={{0,448},{64,0},{128,64},{192,128},{256,192},{320,256},{384,320},{4... | collective-permute-start | bytes 1032200 | tf_op jit(solution)/shard_map/ppermute | solution.py:26
  71.8 10.3 %collective-permute-start.4 = (bf16[448,384]{1,0:T(8,128)(2,1)S(1)}, bf16[448,384]{1,0:T(8,128)(2,1)S(1)}, u32[]{:S(2)}, u32[]{:S(2)}) collective-permute-start(bf16[448,384]{1,0:T(8,128)(2,1)S(1)} %collective-permute-done.2), channel_id=1, source_target_pairs={{0,64},{64,128},{128,192},{192,256},{256,320},{320,384},{384,448},... | collective-permute-start | bytes 1032200 | tf_op jit(solution)/shard_map/ppermute | solution.py:23
  75.3 10.4 %collective-permute-start.5 = (bf16[448,384]{1,0:T(8,128)(2,1)S(1)}, bf16[448,384]{1,0:T(8,128)(2,1)S(1)}, u32[]{:S(2)}, u32[]{:S(2)}) collective-permute-start(bf16[448,384]{1,0:T(8,128)(2,1)S(1)} %collective-permute-done.3), channel_id=1, source_target_pairs={{0,448},{64,0},{128,64},{192,128},{256,192},{320,256},{384,320},{4... | collective-permute-start | bytes 1032200 | tf_op jit(solution)/shard_map/ppermute | solution.py:26
  82.2 10.3 %collective-permute-start.6 = (bf16[448,384]{1,0:T(8,128)(2,1)S(1)}, bf16[448,384]{1,0:T(8,128)(2,1)S(1)}, u32[]{:S(2)}, u32[]{:S(2)}) collective-permute-start(bf16[448,384]{1,0:T(8,128)(2,1)S(1)} %collective-permute-done.4), channel_id=1, source_target_pairs={{0,64},{64,128},{128,192},{192,256},{256,320},{320,384},{384,448},... | collective-permute-start | bytes 1032200 | tf_op jit(solution)/shard_map/ppermute | solution.py:23
  96.3 4.9 %copy-start.1 = (bf16[8,48,3584]{2,1,0:T(8,128)(2,1)}, bf16[8,48,3584]{2,1,0:T(8,128)(2,1)S(1)}, u32[]{:S(2)}) copy-start(bf16[8,48,3584]{2,1,0:T(8,128)(2,1)S(1)} %get-tuple-element.26) | copy-start | bytes 8257540
  96.3 4.9 %copy-start.3 = (bf16[8,48,3584]{2,1,0:T(8,128)(2,1)}, bf16[8,48,3584]{2,1,0:T(8,128)(2,1)S(1)}, u32[]{:S(2)}) copy-start(bf16[8,48,3584]{2,1,0:T(8,128)(2,1)S(1)} %get-tuple-element.27) | copy-start | bytes 8257540
  112.2 96.5 %reduce-scatter.7.cloned.1.call-start = ((), (), s32[]{:S(2)}) async-start(), calls=%async_computation.6 | async-start | bytes 3096576
  112.3 2.6 %copy-start.2 = (bf16[8,48,3584]{2,1,0:T(8,128)(2,1)S(1)}, bf16[8,48,3584]{2,1,0:T(8,128)(2,1)}, u32[]{:S(2)}) copy-start(bf16[8,48,3584]{2,1,0:T(8,128)(2,1)} %copy-done.1) | copy-start | bytes 8257540
  122.6 88.3 %copy-start.7 = (s32[128,8]{0,1:T(8,128)S(1)}, s32[128,8]{0,1:T(8,128)}, u32[]{:S(2)}) copy-start(s32[128,8]{0,1:T(8,128)} %param.9) | copy-start | bytes 12292
  157.1 53.4 %all-to-all-start.1 = ((bf16[8,16,3584]{2,1,0:T(8,128)(2,1)}), bf16[8,16,3584]{2,1,0:T(8,128)(2,1)S(1)}, u32[]{:S(2)}, u32[]{:S(2)}) async-start(bf16[8,16,3584]{2,1,0:T(8,128)(2,1)} %bitcast.12), calls=%async_computation.2 | async-start | bytes 1835008 | tf_op jit(solution)/shard_map/all_to_all | solution.py:108
Sparse Core Ops, SparseCore 0:
  44.8 42.2 all-gather.2
  112.3 42.1 reduce-scatter.4
  157.4 51.3 reduce-scatter.6
